TPU v7x, 32 devices: a whole 2x2x4 slice. The times are simulated.
32 devices in a mesh: rows: 16 (over z, y, x), cols: 2 (over core).
Axes of the slice: x: 2, y: 2, z: 4, core: 2. Of those that a mesh axis runs over, the one named last changes fastest.
Arguments:
- tokens_in: bfloat16 [6304, 768], P(('rows', 'cols')), may hold values from -6 to 6
- ln1_gain: float32 [768], replicated, may hold values from 0.5 to 1.5
- ln1_shift: float32 [768], replicated, may hold values from -4 to 4
- qkv_weight: bfloat16 [768, 2304], P(None, 'cols'), may hold values from -0.21875 to 0.21875
- out_weight: bfloat16 [768, 768], P('cols'), may hold values from -1.75 to 1.75
- ln2_gain: float32 [768], replicated, may hold values from 0.5 to 1.5
- ln2_shift: float32 [768], replicated, may hold values from -4 to 4
- router_weight: bfloat16 [768, 32], replicated, may hold values from -0.4375 to 0.4375
- expert_in: bfloat16 [768, 98304], P(None, ('rows', 'cols')), may hold values from -0.21875 to 0.21875
- expert_out: bfloat16 [98304, 768], P(('rows', 'cols')), may hold values from -0.4375 to 0.4375
- routes: int32 [6304, 2], P(('rows', 'cols')), may hold values from 0 to 31, all different within a row; in each aligned block of 197 rows (0 to 196, 197 to 393, ...) at most 16 rows name the same one
- cotangent: bfloat16 [6304, 768], P(('rows', 'cols')), may hold values from -6 to 6
Outputs:
- output: bfloat16 [6304, 768], P(('rows', 'cols'))
- tokens_grad: bfloat16 [6304, 768], P(('rows', 'cols'))
- ln1_gain_grad: float32 [768], replicated
- ln1_shift_grad: float32 [768], replicated
- qkv_grad: float32 [768, 2304], P(None, 'cols')
- out_grad: float32 [768, 768], P('cols')
- ln2_gain_grad: float32 [768], replicated
- ln2_shift_grad: float32 [768], replicated
- router_grad: float32 [768, 32], replicated
- expert_in_grad: float32 [768, 98304], P(None, ('rows', 'cols'))
- expert_out_grad: float32 [98304, 768], P(('rows', 'cols'))
Inputs may be any that keep to these rules, and one draw needn't show every extreme that they name: `routes`: the two experts of a token differ. Among the tokens of one device (aligned blocks of 197 rows) each expert is named by at most 16 assignments, a bound that some block reaches.
All inputs are finite; a program needn't handle non-finite values.
Results may differ from a plain program's by a relative error of at most 0.022.
Values may be sent and summed in bfloat16 or wider, within the bound.
A program may use at most 192 MiB of HBM per device.

v0:
```python
import jax
import jax.numpy as jnp
from jax import lax
from jax.sharding import PartitionSpec as P

DH = 64
FF = 3072
SEQ = 197
EPSILON = 1e-06


def layer_norm(values, norm_gain, norm_shift):
    average = jnp.mean(values, axis=-1, keepdims=True)
    centred = values - average
    variance = jnp.mean(centred * centred, axis=-1, keepdims=True)
    return centred * lax.rsqrt(variance + EPSILON) * norm_gain + norm_shift


def gelu_slope(pre_act):
    normal_cdf = 0.5 * (1.0 + jax.scipy.special.erf(pre_act * 0.7071067811865476))
    density = jnp.exp(-0.5 * pre_act * pre_act) * 0.3989422804014327
    return normal_cdf + pre_act * density


def dot_rows(first_side, second_side):
    return lax.dot_general(
        first_side, second_side, (((0,), (0,)), ((), ())), preferred_element_type=jnp.float32
    )


def dot_last(first_side, second_side):
    return lax.dot_general(
        first_side, second_side, (((1,), (1,)), ((), ())), preferred_element_type=jnp.float32
    )


def attention_scores(queries, keys_all, score_scale):
    scores = jnp.einsum("nqhd,nkhd->nhqk", queries, keys_all, preferred_element_type=jnp.float32)
    return scores * score_scale


def body(
    tokens_in,
    ln1_gain,
    ln1_shift,
    qkv_weight,
    out_weight,
    ln2_gain,
    ln2_shift,
    router_weight,
    expert_in,
    expert_out,
    routes,
    cotangent,
):
    local_rows = tokens_in.shape[0]
    model_width = tokens_in.shape[1]
    experts = router_weight.shape[1]
    capacity = max(2, 8 * local_rows // (3 * experts))
    heads_local = qkv_weight.shape[1] // (3 * DH)
    score_scale = DH ** (-0.5)
    row_count = lax.axis_size("rows")
    row_place = lax.axis_index("rows")
    col_place = lax.axis_index("cols")
    per_device = max(1, experts // row_count)
    copies = max(1, row_count // experts)
    slots = per_device * capacity
    piece_half = expert_in.shape[1]
    piece_whole = piece_half * lax.axis_size("cols")
    arrived_rows = row_count * slots
    tokens_f = tokens_in.astype(jnp.float32)
    normed_low = layer_norm(tokens_f, ln1_gain, ln1_shift).astype(jnp.bfloat16)
    gathered = lax.all_gather(normed_low, "cols", axis=0, tiled=True)
    pair_rows = gathered.shape[0]
    images = pair_rows // SEQ
    qkv_low = jnp.dot(gathered, qkv_weight, preferred_element_type=jnp.float32).astype(jnp.bfloat16)
    head_split = qkv_low.reshape(images, SEQ, heads_local, 3, DH)
    queries = head_split[:, :, :, 0]
    keys_all = head_split[:, :, :, 1]
    values_all = head_split[:, :, :, 2]
    scores = attention_scores(queries, keys_all, score_scale)
    score_peak = jnp.max(scores, axis=-1, keepdims=True)
    log_total = score_peak + jnp.log(jnp.sum(jnp.exp(scores - score_peak), axis=-1, keepdims=True))
    weights_low = jnp.exp(scores - log_total).astype(jnp.bfloat16)
    context = jnp.einsum(
        "nhqk,nkhd->nqhd", weights_low, values_all, preferred_element_type=jnp.float32
    )
    context_low = context.astype(jnp.bfloat16).reshape(pair_rows, heads_local * DH)
    row_block = context_low
    attn_out = lax.psum_scatter(
        jnp.dot(row_block, out_weight, preferred_element_type=jnp.float32),
        "cols",
        scatter_dimension=0,
        tiled=True,
    )
    hidden_one = tokens_f + attn_out
    mixed_low = layer_norm(hidden_one, ln2_gain, ln2_shift).astype(jnp.bfloat16)
    logits = jnp.dot(mixed_low, router_weight, preferred_element_type=jnp.float32)
    router_probs = jax.nn.softmax(logits, axis=-1)
    expert_ids = jnp.arange(experts, dtype=jnp.int32)
    chosen = (routes[:, :, None] == expert_ids[None, None, :]).astype(jnp.float32)
    gate_values = jnp.sum(router_probs[:, None, :] * chosen, axis=-1)
    flat_ids = routes.reshape(-1)
    flat_hot = (flat_ids[:, None] == expert_ids[None, :]).astype(jnp.int32)
    slot_ranks = jnp.sum(jnp.cumsum(flat_hot, axis=0) * flat_hot, axis=1) - 1
    first_device = flat_ids // per_device * copies
    slot_index = flat_ids % per_device * capacity + slot_ranks
    copy_ids = jnp.arange(copies, dtype=jnp.int32)
    targets = ((first_device[:, None] + copy_ids[None, :]) * slots + slot_index[:, None]).reshape(
        -1
    )
    grad_out = cotangent.astype(jnp.float32)
    grad_slots = (
        (gate_values[:, :, None] * grad_out[:, None, :])
        .astype(jnp.bfloat16)
        .reshape(2 * local_rows, model_width)
    )
    rows_send = (
        jnp.zeros((arrived_rows, model_width), jnp.bfloat16)
        .at[targets]
        .set(jnp.repeat(mixed_low, 2 * copies, axis=0))
    )
    grads_send = (
        jnp.zeros((arrived_rows, model_width), jnp.bfloat16)
        .at[targets]
        .set(jnp.repeat(grad_slots, copies, axis=0))
    )
    arrived, grad_result = (
        lax.all_to_all(
            rows_send.reshape(row_count, slots, model_width),
            "rows",
            split_axis=0,
            concat_axis=0,
            tiled=True,
        ),
        lax.all_to_all(
            grads_send.reshape(row_count, slots, model_width),
            "rows",
            split_axis=0,
            concat_axis=0,
            tiled=True,
        ),
    )
    arrived = arrived.reshape(arrived_rows, model_width)
    grad_result = grad_result.reshape(arrived_rows, model_width)
    unit_base = row_place % copies * piece_whole
    both_rows, both_grads = (
        lax.all_gather(arrived, "cols", axis=0, tiled=True),
        lax.all_gather(grad_result, "cols", axis=0, tiled=True),
    )
    slot_local = jnp.arange(both_rows.shape[0], dtype=jnp.int32) % slots // capacity
    unit_local = (
        unit_base + col_place * piece_half + jnp.arange(piece_half, dtype=jnp.int32)
    ) // FF
    mask = (slot_local[:, None] == unit_local[None, :]).astype(jnp.float32)
    pre_act = jnp.dot(both_rows, expert_in, preferred_element_type=jnp.float32) * mask
    act_low = jax.nn.gelu(pre_act, approximate=False).astype(jnp.bfloat16)
    result_low = lax.psum_scatter(
        jnp.dot(act_low, expert_out, preferred_element_type=jnp.float32).astype(jnp.bfloat16),
        "cols",
        scatter_dimension=0,
        tiled=True,
    )
    grad_act = dot_last(both_grads, expert_out)
    grad_pre_low = (grad_act * gelu_slope(pre_act) * mask).astype(jnp.bfloat16)
    first_grad = dot_rows(both_rows, grad_pre_low)
    second_grad = dot_rows(act_low, both_grads)
    grad_arrived = lax.psum_scatter(
        dot_last(grad_pre_low, expert_in).astype(jnp.bfloat16),
        "cols",
        scatter_dimension=0,
        tiled=True,
    )
    returned = lax.all_to_all(
        result_low.reshape(row_count, slots, model_width),
        "rows",
        split_axis=0,
        concat_axis=0,
        tiled=True,
    )
    returned = returned.reshape(arrived_rows, model_width)
    picked = jnp.sum(
        returned[targets].reshape(local_rows, 2, copies, model_width).astype(jnp.float32), axis=2
    )
    output = (hidden_one + jnp.sum(gate_values[:, :, None] * picked, axis=1)).astype(jnp.bfloat16)
    grad_gates = jnp.sum(grad_out[:, None, :] * picked, axis=-1)
    grad_sent = lax.all_to_all(
        grad_arrived.reshape(row_count, slots, model_width),
        "rows",
        split_axis=0,
        concat_axis=0,
        tiled=True,
    )
    grad_sent = grad_sent.reshape(arrived_rows, model_width)
    grad_mixed_experts = jnp.sum(
        grad_sent[targets].reshape(local_rows, 2 * copies, model_width).astype(jnp.float32), axis=1
    )
    gate_term = jnp.sum(grad_gates * gate_values, axis=-1, keepdims=True)
    grad_probs = jnp.sum(chosen * grad_gates[:, :, None], axis=1)
    grad_logits_low = (router_probs * (grad_probs - gate_term)).astype(jnp.bfloat16)
    router_grad = dot_rows(mixed_low, grad_logits_low)
    grad_mixed = dot_last(grad_logits_low, router_weight) + grad_mixed_experts
    unused_two, norm_two_back = jax.vjp(layer_norm, hidden_one, ln2_gain, ln2_shift)
    grad_hidden_part, ln2_gain_grad, ln2_shift_grad = norm_two_back(grad_mixed)
    grad_hidden = grad_out + grad_hidden_part
    grad_attn_low = grad_hidden.astype(jnp.bfloat16)
    grad_attn_all = lax.all_gather(grad_attn_low, "cols", axis=0, tiled=True)
    out_grad = dot_rows(context_low, grad_attn_all)
    grad_context = (
        dot_last(grad_attn_all, out_weight)
        .astype(jnp.bfloat16)
        .reshape(images, SEQ, heads_local, DH)
    )
    scores_again = attention_scores(queries, keys_all, score_scale)
    attn_probs = jnp.exp(scores_again - log_total)
    probs_low = attn_probs.astype(jnp.bfloat16)
    grad_values = jnp.einsum(
        "nhqk,nqhd->nkhd", probs_low, grad_context, preferred_element_type=jnp.float32
    )
    grad_weights = jnp.einsum(
        "nqhd,nkhd->nhqk", grad_context, values_all, preferred_element_type=jnp.float32
    )
    row_term = jnp.sum(grad_weights * attn_probs, axis=-1, keepdims=True)
    grad_scores = (attn_probs * (grad_weights - row_term)).astype(jnp.bfloat16)
    grad_queries = (
        jnp.einsum("nhqk,nkhd->nqhd", grad_scores, keys_all, preferred_element_type=jnp.float32)
        * score_scale
    )
    grad_keys = (
        jnp.einsum("nhqk,nqhd->nkhd", grad_scores, queries, preferred_element_type=jnp.float32)
        * score_scale
    )
    grad_qkv = (
        jnp.stack([grad_queries, grad_keys, grad_values], axis=3)
        .astype(jnp.bfloat16)
        .reshape(pair_rows, 3 * heads_local * DH)
    )
    qkv_grad = dot_rows(gathered, grad_qkv)
    row_block = grad_qkv
    grad_normed = lax.psum_scatter(
        dot_last(row_block, qkv_weight).astype(jnp.bfloat16),
        "cols",
        scatter_dimension=0,
        tiled=True,
    ).astype(jnp.float32)
    unused_one, norm_one_back = jax.vjp(layer_norm, tokens_f, ln1_gain, ln1_shift)
    grad_tokens_part, ln1_gain_grad, ln1_shift_grad = norm_one_back(grad_normed)
    tokens_grad = (grad_hidden + grad_tokens_part).astype(jnp.bfloat16)
    qkv_grad, out_grad = lax.psum((qkv_grad, out_grad), "rows")
    router_grad, ln1_gain_grad, ln1_shift_grad, ln2_gain_grad, ln2_shift_grad = lax.psum(
        (router_grad, ln1_gain_grad, ln1_shift_grad, ln2_gain_grad, ln2_shift_grad),
        ("rows", "cols"),
    )
    return (
        output,
        tokens_grad,
        ln1_gain_grad,
        ln1_shift_grad,
        qkv_grad,
        out_grad,
        ln2_gain_grad,
        ln2_shift_grad,
        router_grad,
        first_grad,
        second_grad,
    )


def solution(mesh):
    in_specs = (
        P(("rows", "cols"), None),
        P(),
        P(),
        P(None, "cols"),
        P("cols", None),
        P(),
        P(),
        P(),
        P(None, ("rows", "cols")),
        P(("rows", "cols"), None),
        P(("rows", "cols"), None),
        P(("rows", "cols"), None),
    )
    out_specs = (
        P(("rows", "cols"), None),
        P(("rows", "cols"), None),
        P(),
        P(),
        P(None, "cols"),
        P("cols", None),
        P(),
        P(),
        P(),
        P(None, ("rows", "cols")),
        P(("rows", "cols"), None),
    )
    return jax.shard_map(body, mesh=mesh, in_specs=in_specs, out_specs=out_specs, check_vma=False)
```

profile of v0, /device:TPU:0, one launch (start us, length us, event | category | flops | bytes accessed | tf_op | source)
XLA Modules:
  0.0 595.0 jit_solution(453533763309978735)
XLA Ops:
  7.2 1.2 convert_reduce_fusion.1
  8.4 1.2 fusion.33
  10.2 1.2 fusion.50
  11.4 2.3 all-gather
  14.9 2.8 reshape.405
  17.7 7.0 %fusion.72 = (bf16[2,197,6,1,64]{4,3,2,1,0:T(2,128)(2,1)S(1)}, bf16[2,197,6,1,64]{4,3,2,1,0:T(2,128)(2,1)}, bf16[2,197,6,1,64]{4,3,2,1,0:T(2,128)(2,1)}) fusion(bf16[2,197,6,3,64]{4,3,2,1,0:T(4,128)(2,1)} %reshape.405), kind=kLoop, calls=%fused_computation.161 | loop fusion | bytes 1815552 | tf_op jit(solution)/shard_map/slice | solution.py:78
  24.7 2.5 copy.120
  27.2 3.7 copy.122
  30.9 2.0 copy.121
  32.9 1.7 multiply_reduce_fusion.1
  38.1 1.7 fusion.74
  39.8 4.9 fusion
  45.4 2.0 collective-permute-start
  48.0 1.2 reduce-window.6
  50.8 2.1 concatenate
  54.5 1.7 reshape.387
  56.2 3.9 scatter_custom_fusion
  60.0 8.3 %all-to-all-start = ((bf16[16,32,768]{2,1,0:T(8,128)(2,1)}), bf16[16,32,768]{2,1,0:T(8,128)(2,1)}, u32[]{:S(2)}, u32[]{:S(2)}) async-start(bf16[16,32,768]{2,1,0:T(8,128)(2,1)} %bitcast.8), calls=%async_computation | async-start | bytes 1572864 | tf_op jit(solution)/shard_map/all_to_all | solution.py:129
  68.4 1.3 mul.301
  69.7 2.1 mul.309
  72.2 15.5 %all-to-all-done = bf16[16,32,768]{2,1,0:T(8,128)(2,1)} async-done(((bf16[16,32,768]{2,1,0:T(8,128)(2,1)}), bf16[16,32,768]{2,1,0:T(8,128)(2,1)}, u32[]{:S(2)}, u32[]{:S(2)}) %all-to-all-start) | async-done | bytes 786464 | tf_op jit(solution)/shard_map/all_to_all | solution.py:129
  88.0 3.2 scatter_custom_fusion.1
  91.2 4.9 all-to-all-start.2
  96.2 18.6 %all-to-all-done.2 = bf16[16,32,768]{2,1,0:T(8,128)(2,1)S(1)} async-done(((bf16[16,32,768]{2,1,0:T(8,128)(2,1)}), bf16[16,32,768]{2,1,0:T(8,128)(2,1)S(1)}, u32[]{:S(2)}, u32[]{:S(2)}) %all-to-all-start.2) | async-done | bytes 786464 | tf_op jit(solution)/shard_map/all_to_all | solution.py:136
  115.8 35.3 %fusion.5 = (bf16[1024,3072]{1,0:T(8,128)(2,1)S(1)}, f32[1024,3072]{1,0:T(8,128)}) fusion(s32[3072]{0:T(1024)S(1)} %add_select_fusion, s32[1024]{0:T(1024)S(1)} %add_select_fusion.1, bf16[1024,768]{1,0:T(8,128)(2,1)} %all-gather.5.cloned.1.call-done, bf16[768,3072]{1,0:T(8,128)(2,1)} %param.20), kind=kOutput, calls=%fused_computation.11 | convolution fusion | flops 5042601984 | bytes 25182208 | tf_op jit(solution)/shard_map/dot_general | solution.py:156
  151.1 2.7 copy-done.44
  153.8 8.5 %convolution_convert_fusion.2 = bf16[1024,768]{1,0:T(8,128)(2,1)} fusion(bf16[1024,3072]{1,0:T(8,128)(2,1)S(1)} %get-tuple-element.37, bf16[3072,768]{1,0:T(8,128)(2,1)} %param.21), kind=kOutput, calls=%fused_computation.39 | convolution fusion | flops 4832624640 | bytes 12582912 | tf_op jit(solution)/shard_map/dot_general | solution.py:159
  162.3 8.7 %reduce-scatter.9.cloned.1.call-start = ((), (), s32[]{:S(2)}) async-start(), calls=%async_computation.9 | async-start | bytes 2359296 | tf_op jit(solution)/shard_map/reduce_scatter | solution.py:168
  171.1 12.0 %fusion.2 = bf16[1024,3072]{1,0:T(8,128)(2,1)S(1)} fusion(f32[1024,3072]{1,0:T(8,128)} %get-tuple-element.38, bf16[1024,768]{1,0:T(8,128)(2,1)} %all-gather.7.cloned.1.call-done, bf16[3072,768]{1,0:T(8,128)(2,1)} %param.21, s32[3072]{0:T(1024)S(1)} %add_select_fusion, s32[1024]{0:T(1024)S(1)} %add_select_fusion.1), kind=kOutput, calls=%fused_computation.8 | convolution fusion | flops 4872732672 | bytes 25182208 | tf_op jit(solution)/shard_map/dot_general | solution.py:32
  183.1 2.7 copy-done.43
  185.8 6.3 %convolution_convert_fusion.1 = bf16[1024,768]{1,0:T(8,128)(2,1)} fusion(bf16[1024,3072]{1,0:T(8,128)(2,1)S(1)} %fusion.2, bf16[768,3072]{1,0:T(8,128)(2,1)S(1)} %bitcast.115), kind=kOutput, calls=%fused_computation.38 | convolution fusion | flops 4832624640 | bytes 12582912 | tf_op jit(solution)/shard_map/dot_general | solution.py:32
  192.1 5.2 all-to-all-start.1
  197.2 3.5 reduce-scatter.9.cloned.1.call-done
  200.8 15.2 %all-to-all-done.1 = bf16[16,32,768]{2,1,0:T(8,128)(2,1)S(1)} async-done(((bf16[16,32,768]{2,1,0:T(8,128)(2,1)}), bf16[16,32,768]{2,1,0:T(8,128)(2,1)S(1)}, u32[]{:S(2)}, u32[]{:S(2)}) %all-to-all-start.1) | async-done | bytes 786464 | tf_op jit(solution)/shard_map/all_to_all | solution.py:174
  216.0 4.9 all-to-all-start.3
  220.9 1.8 convert_element_type.105
  222.8 2.6 gather_fusion
  225.4 2.8 reshape.365
  228.2 4.7 multiply_reduce_fusion.2
  234.1 5.3 all-to-all-done.3
  239.5 2.6 gather_fusion.1
  242.1 2.8 reshape.366
  245.0 2.7 reduce_sum.212
  248.5 1.3 multiply_reduce_fusion.4
  249.8 2.0 fusion.70
  252.8 2.6 all-gather.1
  256.3 1.7 convolution_convert_fusion.6
  258.1 1.3 reshape.406
  259.4 1.5 copy.106
  260.9 3.2 fusion.22
  267.5 1.2 copy.111
  268.7 1.5 convert_element_type.115
  270.2 4.6 fusion.75
  274.9 1.5 fusion.76
  276.4 10.0 %fusion.79 = f32[3072,768]{1,0:T(8,128)} fusion(bf16[1024,3072]{1,0:T(8,128)(2,1)} %copy-done.44, bf16[1024,768]{1,0:T(8,128)(2,1)} %all-gather.7.cloned.1.call-done), kind=kOutput, calls=%fused_computation.168 | convolution fusion | flops 4831838208 | bytes 17301504 | tf_op jit(solution)/shard_map/dot_general | solution.py:26
  286.4 1.2 convolution_convert_fusion.3
  287.7 3.4 fusion.1
  291.8 2.7 collective-permute-start.1
  294.5 9.9 %fusion.78 = f32[768,3072]{1,0:T(8,128)} fusion(bf16[1024,768]{1,0:T(8,128)(2,1)} %all-gather.5.cloned.1.call-done, bf16[1024,3072]{1,0:T(8,128)(2,1)} %copy-done.43), kind=kOutput, calls=%fused_computation.167 | convolution fusion | flops 4831838208 | bytes 17301504 | tf_op jit(solution)/shard_map/dot_general | solution.py:26
  304.4 2.0 concatenate.1
  307.3 40.2 %all-reduce.5 = (f32[768]{0:T(1024)}, f32[768]{0:T(1024)}, f32[768]{0:T(1024)}, f32[768]{0:T(1024)}) all-reduce(f32[768]{0:T(1024)S(1)} %get-tuple-element.15, f32[768]{0:T(1024)S(1)} %get-tuple-element.18, f32[768]{0:T(1024)S(1)} %get-tuple-element.11, ...), channel_id=1, replica_groups=mesh['rows'=16,'cols'=2] {'rows','cols'}, use_global_device_ids=true, to_apply=%region_29.30 | all-reduce | flops 3072 | bytes 24576 | tf_op jit(solution)/shard_map/psum | solution.py:250
  348.6 46.3 %all-reduce.10.cloned.1.call-done = f32[768,32]{0,1:T(8,128)} async-done(((f32[768,32]{0,1:T(8,128)}), f32[768,32]{0,1:T(8,128)}) %all-reduce.10.cloned.1.call-update) | async-done | bytes 98320 | tf_op jit(solution)/shard_map/psum | solution.py:250
  394.8 187.2 %all-reduce.12.cloned.1.call-done = (f32[768,1152]{1,0:T(8,128)}, f32[384,768]{1,0:T(8,128)}) async-done(((f32[768,1152]{1,0:T(8,128)}, f32[384,768]{1,0:T(8,128)}), (f32[768,1152]{1,0:T(8,128)}, f32[384,768]{1,0:T(8,128)})) %all-reduce.12.cloned.1.call-update) | async-done | bytes 4718608 | tf_op jit(solution)/shard_map/psum | solution.py:249
  582.0 4.1 copy.130
  (169 shorter events, 22.3 us)
Async XLA Ops:
  7.2 6.7 %copy-start = (bf16[768,1152]{1,0:T(8,128)(2,1)S(1)}, bf16[768,1152]{1,0:T(8,128)(2,1)}, u32[]{:S(2)}) copy-start(bf16[768,1152]{1,0:T(8,128)(2,1)} %param.15) | copy-start | bytes 5308420
  8.4 3.0 copy-start.29
  9.6 0.5 copy-start.37
  10.2 1.2 copy-start.32
  13.9 1.0 copy-start.24
  27.2 9.4 %copy-start.13 = (bf16[2,197,6,1,64]{1,4,2,0,3:T(8,128)(2,1)}, bf16[2,197,6,1,64]{1,4,2,0,3:T(8,128)(2,1)S(1)}, u32[]{:S(2)}) copy-start(bf16[2,197,6,1,64]{1,4,2,0,3:T(8,128)(2,1)S(1)} %copy.120) | copy-start | bytes 907780
  34.6 1.4 copy-start.1
  35.1 12.4 %copy-start.31 = (s32[197,2]{0,1:T(2,128)S(1)}, s32[197,2]{0,1:T(2,128)}, u32[]{:S(2)}) copy-start(s32[197,2]{0,1:T(2,128)} %param.22) | copy-start | bytes 4732
  36.0 13.5 %copy-start.42 = (u32[32]{0:T(128)S(1)}, u32[32]{0:T(128)}, u32[]{:S(2)}) copy-start(u32[32]{0:T(128)} %constant.193) | copy-start | bytes 388
  36.0 16.9 %copy-start.5 = (bf16[197,768]{1,0:T(8,128)(2,1)S(1)}, bf16[197,768]{1,0:T(8,128)(2,1)}, u32[]{:S(2)}) copy-start(bf16[197,768]{1,0:T(8,128)(2,1)} %param.12) | copy-start | bytes 907780
  37.1 16.9 %copy-start.28 = (f32[768]{0:T(1024)S(1)}, f32[768]{0:T(1024)}, u32[]{:S(2)}) copy-start(f32[768]{0:T(1024)} %param.17) | copy-start | bytes 9220
  37.1 16.9 %copy-start.41 = (f32[768]{0:T(1024)S(1)}, f32[768]{0:T(1024)}, u32[]{:S(2)}) copy-start(f32[768]{0:T(1024)} %param.18) | copy-start | bytes 9220
  45.4 5.4 collective-permute-start
  47.9 20.5 %copy-start.9 = (bf16[197,768]{1,0:T(8,128)(2,1)S(1)}, bf16[197,768]{1,0:T(8,128)(2,1)}, u32[]{:S(2)}) copy-start(bf16[197,768]{1,0:T(8,128)(2,1)} %param.23) | copy-start | bytes 907780
  53.1 0.8 copy-start.3
  53.4 18.8 %copy-start.39 = (f32[197]{0:T(256)}, f32[197]{0:T(256)S(1)}, u32[]{:S(2)}) copy-start(f32[197]{0:T(256)S(1)} %multiply_reduce_fusion.6) | copy-start | bytes 2368
  53.4 18.5 %copy-start.25 = (bf16[768,32]{0,1:T(8,128)(2,1)S(1)}, bf16[768,32]{0,1:T(8,128)(2,1)}, u32[]{:S(2)}) copy-start(bf16[768,32]{0,1:T(8,128)(2,1)} %param.19) | copy-start | bytes 147460
  53.9 18.2 %copy-start.34 = (f32[197]{0:T(256)}, f32[197]{0:T(256)S(1)}, u32[]{:S(2)}) copy-start(f32[197]{0:T(256)S(1)} %fusion.67) | copy-start | bytes 2368
  54.1 33.6 %copy-start.11 = (bf16[197,768]{1,0:T(8,128)(2,1)}, bf16[197,768]{1,0:T(8,128)(2,1)S(1)}, u32[]{:S(2)}) copy-start(bf16[197,768]{1,0:T(8,128)(2,1)S(1)} %add_convert_fusion.2) | copy-start | bytes 907780
  60.0 27.7 %all-to-all-start = ((bf16[16,32,768]{2,1,0:T(8,128)(2,1)}), bf16[16,32,768]{2,1,0:T(8,128)(2,1)}, u32[]{:S(2)}, u32[]{:S(2)}) async-start(bf16[16,32,768]{2,1,0:T(8,128)(2,1)} %bitcast.8), calls=%async_computation | async-start | bytes 1572864 | tf_op jit(solution)/shard_map/all_to_all | solution.py:129
  68.3 47.4 %all-gather.5.cloned.1.call-start = ((), (), s32[]{:S(2)}) async-start(), calls=%async_computation.6 | async-start | bytes 2359296 | tf_op jit(solution)/shard_map/all_gather | solution.py:148
  72.2 15.5 %copy-start.36 = (f32[197]{0:T(256)}, f32[197]{0:T(256)S(1)}, u32[]{:S(2)}) copy-start(f32[197]{0:T(256)S(1)} %fusion.55) | copy-start | bytes 2368
  91.2 23.5 %all-to-all-start.2 = ((bf16[16,32,768]{2,1,0:T(8,128)(2,1)}), bf16[16,32,768]{2,1,0:T(8,128)(2,1)S(1)}, u32[]{:S(2)}, u32[]{:S(2)}) async-start(bf16[16,32,768]{2,1,0:T(8,128)(2,1)} %bitcast.107), calls=%async_computation.3 | async-start | bytes 1572864 | tf_op jit(solution)/shard_map/all_to_all | solution.py:136
  96.1 74.9 %all-gather.7.cloned.1.call-start = ((), (), s32[]{:S(2)}) async-start(), calls=%async_computation.8 | async-start | bytes 2359296 | tf_op jit(solution)/shard_map/all_gather | solution.py:149
  114.8 0.9 copy-start.18
  115.7 76.4 %reduce-scatter.7.cloned.1.call-start = ((), (), s32[]{:S(2)}) async-start(), calls=%async_computation.7 | async-start | bytes 2359296 | tf_op jit(solution)/shard_map/reduce_scatter | solution.py:158
  151.0 2.7 copy-start.44
  153.8 32.0 %slice-start = ((s8[4718592]{0:T(1024)(128)(4,1)}), s8[524288]{0:T(1024)(128)(4,1)S(1)}, s32[]{:S(2)}) async-start(s8[4718592]{0:T(1024)(128)(4,1)} %bitcast.114), calls=%async_computation.12 | async-start | bytes 1048576
  162.3 38.5 %reduce-scatter.9.cloned.1.call-start = ((), (), s32[]{:S(2)}) async-start(), calls=%async_computation.9 | async-start | bytes 2359296 | tf_op jit(solution)/shard_map/reduce_scatter | solution.py:168
  171.1 14.7 %slice-start.1 = ((s8[4718592]{0:T(1024)(128)(4,1)}), s8[4194304]{0:T(1024)(128)(4,1)S(1)}, s32[]{:S(2)}) async-start(s8[4718592]{0:T(1024)(128)(4,1)} %bitcast.114), calls=%async_computation.13 | async-start | bytes 8388608
  183.1 2.7 copy-start.43
  192.1 23.9 %all-to-all-start.1 = ((bf16[16,32,768]{2,1,0:T(8,128)(2,1)}), bf16[16,32,768]{2,1,0:T(8,128)(2,1)S(1)}, u32[]{:S(2)}, u32[]{:S(2)}) async-start(bf16[16,32,768]{2,1,0:T(8,128)(2,1)} %bitcast.109), calls=%async_computation.2 | async-start | bytes 1572864 | tf_op jit(solution)/shard_map/all_to_all | solution.py:174
  216.0 23.5 %all-to-all-start.3 = ((bf16[16,32,768]{2,1,0:T(8,128)(2,1)}), bf16[16,32,768]{2,1,0:T(8,128)(2,1)S(1)}, u32[]{:S(2)}, u32[]{:S(2)}) async-start(bf16[16,32,768]{2,1,0:T(8,128)(2,1)} %bitcast.108), calls=%async_computation.5 | async-start | bytes 1572864 | tf_op jit(solution)/shard_map/all_to_all | solution.py:187
  220.9 174.0 %all-reduce.10.cloned.1.call-start = ((), (), s32[]{:S(2)}) async-start(), calls=%async_computation.10 | async-start | bytes 196608 | tf_op jit(solution)/shard_map/psum | solution.py:250
  232.8 15.6 %copy-start.4 = (f32[197,768]{1,0:T(8,128)S(1)}, f32[197,768]{1,0:T(8,128)}, u32[]{:S(2)}) copy-start(f32[197,768]{1,0:T(8,128)} %copy-done.3) | copy-start | bytes 1815556
  242.1 7.6 %copy-start.40 = (f32[197]{0:T(256)S(1)}, f32[197]{0:T(256)}, u32[]{:S(2)}) copy-start(f32[197]{0:T(256)} %copy-done.39) | copy-start | bytes 2368
  242.1 7.7 %copy-start.35 = (f32[197]{0:T(256)S(1)}, f32[197]{0:T(256)}, u32[]{:S(2)}) copy-start(f32[197]{0:T(256)} %copy-done.34) | copy-start | bytes 2368
  242.1 10.5 %copy-start.10 = (bf16[197,768]{1,0:T(8,128)(2,1)S(1)}, bf16[197,768]{1,0:T(8,128)(2,1)}, u32[]{:S(2)}) copy-start(bf16[197,768]{1,0:T(8,128)(2,1)} %param.23) | copy-start | bytes 907780
  251.8 0.8 copy-start.7
  252.8 11.3 %copy-start.14 = (bf16[2,197,6,1,64]{1,4,2,0,3:T(8,128)(2,1)S(1)}, bf16[2,197,6,1,64]{1,4,2,0,3:T(8,128)(2,1)}, u32[]{:S(2)}) copy-start(bf16[2,197,6,1,64]{1,4,2,0,3:T(8,128)(2,1)} %copy-done.13) | copy-start | bytes 907780
  260.9 3.2 copy-start.2
  264.1 1.4 copy-start.16
  264.9 1.1 copy-start.15
  264.9 1.5 copy-start.12
  264.9 2.3 copy-start.20
  270.2 4.7 copy-start.17
  270.2 4.7 copy-start.19
  274.9 307.1 %all-reduce.12.cloned.1.call-start = ((), (), s32[]{:S(2)}) async-start(), calls=%async_computation.11 | async-start | bytes 9437184 | tf_op jit(solution)/shard_map/psum | solution.py:249
  276.4 10.0 %copy-start.23 = (bf16[394,1152]{0,1:T(8,128)(2,1)S(1)}, bf16[394,1152]{0,1:T(8,128)(2,1)}, u32[]{:S(2)}) copy-start(bf16[394,1152]{0,1:T(8,128)(2,1)} %convert_element_type.115) | copy-start | bytes 2723332
  291.0 0.7 copy-start.21
  291.8 14.7 %copy-start.6 = (bf16[197,768]{1,0:T(8,128)(2,1)S(1)}, bf16[197,768]{1,0:T(8,128)(2,1)}, u32[]{:S(2)}) copy-start(bf16[197,768]{1,0:T(8,128)(2,1)} %param.12) | copy-start | bytes 907780
  291.8 14.7 %copy-start.27 = (f32[768]{0:T(1024)S(1)}, f32[768]{0:T(1024)}, u32[]{:S(2)}) copy-start(f32[768]{0:T(1024)} %param.13) | copy-start | bytes 9220
  291.8 14.7 %copy-start.30 = (f32[197]{0:T(256)S(1)}, f32[197]{0:T(256)}, u32[]{:S(2)}) copy-start(f32[197]{0:T(256)} %copy-done.29) | copy-start | bytes 2368
  291.8 15.0 %copy-start.38 = (f32[197]{0:T(256)S(1)}, f32[197]{0:T(256)}, u32[]{:S(2)}) copy-start(f32[197]{0:T(256)} %copy-done.37) | copy-start | bytes 2368
  291.8 15.0 %copy-start.33 = (f32[197]{0:T(256)S(1)}, f32[197]{0:T(256)}, u32[]{:S(2)}) copy-start(f32[197]{0:T(256)} %copy-done.32) | copy-start | bytes 2368
  291.8 55.6 %copy-start.8 = (f32[197,768]{1,0:T(8,128)S(1)}, f32[197,768]{1,0:T(8,128)}, u32[]{:S(2)}) copy-start(f32[197,768]{1,0:T(8,128)} %copy-done.7) | copy-start | bytes 1815556
  291.8 12.5 %collective-permute-start.1 = (bf16[3,768]{1,0:T(4,128)(2,1)S(1)}, bf16[3,768]{1,0:T(4,128)(2,1)S(1)}, u32[]{:S(2)}, u32[]{:S(2)}) collective-permute-start(bf16[3,768]{1,0:T(4,128)(2,1)S(1)} %slice.34), channel_id=1, source_target_pairs={{0,1},{2,3},{4,5},{6,7},{8,9},{10,11},{12,13},{14,15},{16,17},{18,... | collective-permute-start | bytes 13832
  582.0 4.1 copy-start.22
  582.0 5.1 copy-start.26
Sparse Core Ops, SparseCore 0:
  87.9 9.0 all-gather.4
  115.8 9.0 all-gather.6
  162.4 8.3 reduce-scatter.6
  192.2 8.5 reduce-scatter.8
  275.0 119.7 all-reduce.9
  401.0 180.9 all-reduce.11
where the time goes:
time: 605 us; the launch traced here: 595 us
  waiting for transfers between devices  292 us (48%)
  matrix products  103 us (17%)
  local copies, waits for them, and re-layouts  68.5 us (11%)
  blocking collectives  53.4 us (9%)
  starting transfers between devices  36.9 us (6%)
  other arithmetic  25.5 us (4%)
  between operations  16.1 us (3%)
    psum x1, waiting for transfers between devices, body(): qkv_grad, out_grad = lax.psum((qkv_grad, out_grad), 'rows')  187 us
    psum x1, waiting for transfers between devices, body(): lax.psum((router_grad, ln1_gain_grad, ln1_shift_grad, ln2_gain_grad, ln2_...  46.3 us
    psum x1, blocking collectives, body(): lax.psum((router_grad, ln1_gain_grad, ln1_shift_grad, ln2_gain_grad, ln2_...  40.2 us
    dot_general x1, matrix products, body(): jnp.dot(both_rows, expert_in, preferred_element_type=jnp.float32) * mask  35.3 us
    unnamed x108, local copies, waits for them, and re-layouts  30.5 us
    dot_general x5, matrix products, dot_rows(): lax.dot_general(first_side, second_side, (((0,), (0,)), ((), ())), prefer...  26.8 us
    dot_general x5, matrix products, dot_last(): lax.dot_general(first_side, second_side, (((1,), (1,)), ((), ())), prefer...  22.5 us
    all_to_all x1, waiting for transfers between devices, body(): lax.all_to_all(grads_send.reshape(row_count, slots, model_width), 'rows',...  18.6 us
  transfers between devices with their start and end apart: 12, of which 7 were waited for; matrix products, arithmetic and copies ran while one was open for 19% of the time, Pallas kernels for 0%

commit v1 on v0

--- a/solution.py
+++ b/solution.py
@@ -248,8 +248,10 @@
     tokens_grad = (grad_hidden + grad_tokens_part).astype(jnp.bfloat16)
     qkv_grad, out_grad = lax.psum((qkv_grad, out_grad), "rows")
     router_grad, ln1_gain_grad, ln1_shift_grad, ln2_gain_grad, ln2_shift_grad = lax.psum(
-        (router_grad, ln1_gain_grad, ln1_shift_grad, ln2_gain_grad, ln2_shift_grad),
-        ("rows", "cols"),
+        lax.psum(
+            (router_grad, ln1_gain_grad, ln1_shift_grad, ln2_gain_grad, ln2_shift_grad), "cols"
+        ),
+        "rows",
     )
     return (
         output,

time: 605 us -> 506 us (0.84)
  waiting for transfers between devices: 292 us -> 152 us
  blocking collectives: 53.4 us -> 94.9 us
    psum x1, waiting for transfers between devices: 187 us -> 77.7 us  [body(): qkv_grad, out_grad = lax.psum((qkv_grad, out_grad), 'rows')]
    psum x0 -> x1, blocking collectives: none -> 78.4 us  [body(): lax.psum(lax.psum((router_grad, ln1_gain_grad, ln1_shift_grad, ln2_gain_g...]
    psum x1, blocking collectives: 40.2 us -> 3.29 us  [body(): lax.psum((router_grad, ln1_gain_grad, ln1_shift_grad, ln2_gain_grad, ln2_...]
    psum x1, waiting for transfers between devices: 46.3 us -> 15.7 us  [body(): lax.psum((router_grad, ln1_gain_grad, ln1_shift_grad, ln2_gain_grad, ln2_...]
  transfers between devices with their start and end apart: 12 -> 12, of which waited for: 7 -> 7; matrix products, arithmetic and copies ran while one was open for 19% -> 23% of each run, Pallas kernels for 0% -> 0%
where the time goes in v1:
time: 506 us; the launch traced here: 497 us
  waiting for transfers between devices  152 us (30%)
  matrix products  103 us (20%)
  blocking collectives  94.9 us (19%)
  local copies, waits for them, and re-layouts  68.5 us (14%)
  starting transfers between devices  36.8 us (7%)
  other arithmetic  25.5 us (5%)
  between operations  16.1 us (3%)
    psum x1, blocking collectives, body(): lax.psum(lax.psum((router_grad, ln1_gain_grad, ln1_shift_grad, ln2_gain_g...  78.4 us
    psum x1, waiting for transfers between devices, body(): qkv_grad, out_grad = lax.psum((qkv_grad, out_grad), 'rows')  77.7 us
    dot_general x1, matrix products, body(): jnp.dot(both_rows, expert_in, preferred_element_type=jnp.float32) * mask  35.3 us
    unnamed x108, local copies, waits for them, and re-layouts  30.6 us
    dot_general x5, matrix products, dot_rows(): lax.dot_general(first_side, second_side, (((0,), (0,)), ((), ())), prefer...  26.8 us
    dot_general x5, matrix products, dot_last(): lax.dot_general(first_side, second_side, (((1,), (1,)), ((), ())), prefer...  22.5 us
    all_to_all x1, waiting for transfers between devices, body(): lax.all_to_all(grads_send.reshape(row_count, slots, model_width), 'rows',...  18.6 us
    psum x1, waiting for transfers between devices, body(): lax.psum((router_grad, ln1_gain_grad, ln1_shift_grad, ln2_gain_grad, ln2_...  15.7 us
  transfers between devices with their start and end apart: 12, of which 7 were waited for; matrix products, arithmetic and copies ran while one was open for 23% of the time, Pallas kernels for 0%

profile of v1, /device:TPU:0, one launch (start us, length us, event | category | flops | bytes accessed | tf_op | source)
XLA Modules:
  0.0 496.6 jit_solution(1925781072087822944)
XLA Ops:
  7.2 1.2 convert_reduce_fusion.1
  8.4 1.2 fusion.33
  10.2 1.2 fusion.50
  11.4 2.3 all-gather
  14.9 2.8 reshape.405
  17.7 7.0 %fusion.72 = (bf16[2,197,6,1,64]{4,3,2,1,0:T(2,128)(2,1)S(1)}, bf16[2,197,6,1,64]{4,3,2,1,0:T(2,128)(2,1)}, bf16[2,197,6,1,64]{4,3,2,1,0:T(2,128)(2,1)}) fusion(bf16[2,197,6,3,64]{4,3,2,1,0:T(4,128)(2,1)} %reshape.405), kind=kLoop, calls=%fused_computation.161 | loop fusion | bytes 1815552 | tf_op jit(solution)/shard_map/slice | solution.py:78
  24.7 2.5 copy.120
  27.2 3.7 copy.122
  30.9 2.0 copy.121
  32.9 1.7 multiply_reduce_fusion.1
  38.1 1.7 fusion.74
  39.8 4.9 fusion
  45.4 2.0 collective-permute-start
  50.8 2.1 concatenate
  54.5 1.7 reshape.387
  56.2 3.9 scatter_custom_fusion
  60.0 8.3 %all-to-all-start = ((bf16[16,32,768]{2,1,0:T(8,128)(2,1)}), bf16[16,32,768]{2,1,0:T(8,128)(2,1)}, u32[]{:S(2)}, u32[]{:S(2)}) async-start(bf16[16,32,768]{2,1,0:T(8,128)(2,1)} %bitcast.8), calls=%async_computation | async-start | bytes 1572864 | tf_op jit(solution)/shard_map/all_to_all | solution.py:129
  68.4 1.3 mul.301
  69.7 2.1 mul.309
  72.2 15.5 %all-to-all-done = bf16[16,32,768]{2,1,0:T(8,128)(2,1)} async-done(((bf16[16,32,768]{2,1,0:T(8,128)(2,1)}), bf16[16,32,768]{2,1,0:T(8,128)(2,1)}, u32[]{:S(2)}, u32[]{:S(2)}) %all-to-all-start) | async-done | bytes 786464 | tf_op jit(solution)/shard_map/all_to_all | solution.py:129
  88.0 3.2 scatter_custom_fusion.1
  91.2 4.9 all-to-all-start.2
  96.2 18.6 %all-to-all-done.2 = bf16[16,32,768]{2,1,0:T(8,128)(2,1)S(1)} async-done(((bf16[16,32,768]{2,1,0:T(8,128)(2,1)}), bf16[16,32,768]{2,1,0:T(8,128)(2,1)S(1)}, u32[]{:S(2)}, u32[]{:S(2)}) %all-to-all-start.2) | async-done | bytes 786464 | tf_op jit(solution)/shard_map/all_to_all | solution.py:136
  115.8 35.3 %fusion.5 = (bf16[1024,3072]{1,0:T(8,128)(2,1)S(1)}, f32[1024,3072]{1,0:T(8,128)}) fusion(s32[3072]{0:T(1024)S(1)} %add_select_fusion, s32[1024]{0:T(1024)S(1)} %add_select_fusion.1, bf16[1024,768]{1,0:T(8,128)(2,1)} %all-gather.5.cloned.1.call-done, bf16[768,3072]{1,0:T(8,128)(2,1)} %param.20), kind=kOutput, calls=%fused_computation.11 | convolution fusion | flops 5042601984 | bytes 25182208 | tf_op jit(solution)/shard_map/dot_general | solution.py:156
  151.1 2.7 copy-done.44
  153.8 8.5 %convolution_convert_fusion.2 = bf16[1024,768]{1,0:T(8,128)(2,1)} fusion(bf16[1024,3072]{1,0:T(8,128)(2,1)S(1)} %get-tuple-element.42, bf16[3072,768]{1,0:T(8,128)(2,1)} %param.21), kind=kOutput, calls=%fused_computation.39 | convolution fusion | flops 4832624640 | bytes 12582912 | tf_op jit(solution)/shard_map/dot_general | solution.py:159
  162.3 8.7 %reduce-scatter.9.cloned.1.call-start = ((), (), s32[]{:S(2)}) async-start(), calls=%async_computation.9 | async-start | bytes 2359296 | tf_op jit(solution)/shard_map/reduce_scatter | solution.py:168
  171.1 12.0 %fusion.2 = bf16[1024,3072]{1,0:T(8,128)(2,1)S(1)} fusion(f32[1024,3072]{1,0:T(8,128)} %get-tuple-element.43, bf16[1024,768]{1,0:T(8,128)(2,1)} %all-gather.7.cloned.1.call-done, bf16[3072,768]{1,0:T(8,128)(2,1)} %param.21, s32[3072]{0:T(1024)S(1)} %add_select_fusion, s32[1024]{0:T(1024)S(1)} %add_select_fusion.1), kind=kOutput, calls=%fused_computation.8 | convolution fusion | flops 4872732672 | bytes 25182208 | tf_op jit(solution)/shard_map/dot_general | solution.py:32
  183.1 2.7 copy-done.43
  185.8 6.3 %convolution_convert_fusion.1 = bf16[1024,768]{1,0:T(8,128)(2,1)} fusion(bf16[1024,3072]{1,0:T(8,128)(2,1)S(1)} %fusion.2, bf16[768,3072]{1,0:T(8,128)(2,1)S(1)} %bitcast.115), kind=kOutput, calls=%fused_computation.38 | convolution fusion | flops 4832624640 | bytes 12582912 | tf_op jit(solution)/shard_map/dot_general | solution.py:32
  192.1 5.2 %all-to-all-start.1 = ((bf16[16,32,768]{2,1,0:T(8,128)(2,1)}), bf16[16,32,768]{2,1,0:T(8,128)(2,1)S(1)}, u32[]{:S(2)}, u32[]{:S(2)}) async-start(bf16[16,32,768]{2,1,0:T(8,128)(2,1)} %bitcast.109), calls=%async_computation.2 | async-start | bytes 1572864 | tf_op jit(solution)/shard_map/all_to_all | solution.py:174
  197.2 3.5 reduce-scatter.9.cloned.1.call-done
  200.8 15.2 %all-to-all-done.1 = bf16[16,32,768]{2,1,0:T(8,128)(2,1)S(1)} async-done(((bf16[16,32,768]{2,1,0:T(8,128)(2,1)}), bf16[16,32,768]{2,1,0:T(8,128)(2,1)S(1)}, u32[]{:S(2)}, u32[]{:S(2)}) %all-to-all-start.1) | async-done | bytes 786464 | tf_op jit(solution)/shard_map/all_to_all | solution.py:174
  216.0 4.9 all-to-all-start.3
  220.9 1.8 convert_element_type.105
  222.8 2.6 gather_fusion
  225.4 2.8 reshape.365
  228.2 4.7 multiply_reduce_fusion.2
  234.1 5.3 %all-to-all-done.3 = bf16[16,32,768]{2,1,0:T(8,128)(2,1)S(1)} async-done(((bf16[16,32,768]{2,1,0:T(8,128)(2,1)}), bf16[16,32,768]{2,1,0:T(8,128)(2,1)S(1)}, u32[]{:S(2)}, u32[]{:S(2)}) %all-to-all-start.3) | async-done | bytes 786464 | tf_op jit(solution)/shard_map/all_to_all | solution.py:187
  239.5 2.6 gather_fusion.1
  242.1 2.8 reshape.366
  245.0 2.7 reduce_sum.212
  248.5 1.3 multiply_reduce_fusion.4
  249.8 2.0 fusion.70
  252.8 2.6 all-gather.1
  256.3 1.7 convolution_convert_fusion.6
  258.1 1.3 reshape.406
  259.4 1.5 copy.106
  260.9 3.2 fusion.22
  267.5 1.2 copy.111
  268.7 1.5 convert_element_type.115
  270.2 4.6 fusion.75
  274.9 1.5 fusion.76
  276.4 15.7 %all-reduce.11.cloned.1.call-done = f32[768,32]{0,1:T(8,128)} async-done(((f32[768,32]{0,1:T(8,128)}), f32[768,32]{0,1:T(8,128)}) %all-reduce.11.cloned.1.call-update) | async-done | bytes 98320 | tf_op jit(solution)/shard_map/psum | solution.py:251
  292.1 10.0 %fusion.79 = f32[3072,768]{1,0:T(8,128)} fusion(bf16[1024,3072]{1,0:T(8,128)(2,1)} %copy-done.44, bf16[1024,768]{1,0:T(8,128)(2,1)} %all-gather.7.cloned.1.call-done), kind=kOutput, calls=%fused_computation.168 | convolution fusion | flops 4831838208 | bytes 17301504 | tf_op jit(solution)/shard_map/dot_general | solution.py:26
  302.2 1.2 convolution_convert_fusion.3
  303.4 3.4 fusion.1
  307.6 2.6 collective-permute-start.1
  310.2 9.9 %fusion.78 = f32[768,3072]{1,0:T(8,128)} fusion(bf16[1024,768]{1,0:T(8,128)(2,1)} %all-gather.5.cloned.1.call-done, bf16[1024,3072]{1,0:T(8,128)(2,1)} %copy-done.43), kind=kOutput, calls=%fused_computation.167 | convolution fusion | flops 4831838208 | bytes 17301504 | tf_op jit(solution)/shard_map/dot_general | solution.py:26
  320.1 2.0 concatenate.1
  323.0 3.3 all-reduce.7
  326.3 78.4 %all-reduce.5 = (f32[768]{0:T(1024)}, f32[768]{0:T(1024)}, f32[768]{0:T(1024)}, f32[768]{0:T(1024)}) all-reduce(f32[768]{0:T(1024)S(1)} %get-tuple-element.26, f32[768]{0:T(1024)S(1)} %get-tuple-element.27, f32[768]{0:T(1024)S(1)} %get-tuple-element.28, f32[768]{0:T(1024)S(1)} %get-tuple-element.29), channel_id=1, replica_groups=mesh['rows'=16,'cols'=2] {'rows'}, use_global_device_ids=true, to_apply=%region_30.31 | all-reduce | flops 3072 | bytes 24576 | tf_op jit(solution)/shard_map/psum | solution.py:250
  405.7 77.7 %all-reduce.13.cloned.1.call-done = (f32[768,1152]{1,0:T(8,128)}, f32[384,768]{1,0:T(8,128)}, f32[768,32]{0,1:T(8,128)}) async-done(((f32[768,1152]{1,0:T(8,128)}, f32[384,768]{1,0:T(8,128)}, f32[768,32]{0,1:T(8,128)}), (f32[768,1152]{1,0:T(8,128)}, f32[384,768]{1,0:T(8,128)}, f32[768,32]{0,1:T(8,128)})) %all-reduce.13.cloned.1.call-update) | async-done | bytes 4816912 | tf_op jit(solution)/shard_map/psum | solution.py:249
  483.5 4.1 copy.131
  (170 shorter events, 23.4 us)
Async XLA Ops:
  7.2 6.7 %copy-start = (bf16[768,1152]{1,0:T(8,128)(2,1)S(1)}, bf16[768,1152]{1,0:T(8,128)(2,1)}, u32[]{:S(2)}) copy-start(bf16[768,1152]{1,0:T(8,128)(2,1)} %param.15) | copy-start | bytes 5308420
  8.4 3.0 copy-start.29
  9.6 0.5 copy-start.37
  10.2 1.2 copy-start.32
  13.9 1.0 copy-start.24
  27.2 9.4 %copy-start.13 = (bf16[2,197,6,1,64]{1,4,2,0,3:T(8,128)(2,1)}, bf16[2,197,6,1,64]{1,4,2,0,3:T(8,128)(2,1)S(1)}, u32[]{:S(2)}) copy-start(bf16[2,197,6,1,64]{1,4,2,0,3:T(8,128)(2,1)S(1)} %copy.120) | copy-start | bytes 907780
  34.6 1.4 copy-start.1
  35.1 12.4 %copy-start.31 = (s32[197,2]{0,1:T(2,128)S(1)}, s32[197,2]{0,1:T(2,128)}, u32[]{:S(2)}) copy-start(s32[197,2]{0,1:T(2,128)} %param.22) | copy-start | bytes 4732
  36.0 13.5 %copy-start.42 = (u32[32]{0:T(128)S(1)}, u32[32]{0:T(128)}, u32[]{:S(2)}) copy-start(u32[32]{0:T(128)} %constant.193) | copy-start | bytes 388
  36.0 16.9 %copy-start.5 = (bf16[197,768]{1,0:T(8,128)(2,1)S(1)}, bf16[197,768]{1,0:T(8,128)(2,1)}, u32[]{:S(2)}) copy-start(bf16[197,768]{1,0:T(8,128)(2,1)} %param.12) | copy-start | bytes 907780
  37.1 16.9 %copy-start.28 = (f32[768]{0:T(1024)S(1)}, f32[768]{0:T(1024)}, u32[]{:S(2)}) copy-start(f32[768]{0:T(1024)} %param.17) | copy-start | bytes 9220
  37.1 16.9 %copy-start.41 = (f32[768]{0:T(1024)S(1)}, f32[768]{0:T(1024)}, u32[]{:S(2)}) copy-start(f32[768]{0:T(1024)} %param.18) | copy-start | bytes 9220
  45.4 5.4 %collective-permute-start = (f32[3,768]{1,0:T(4,128)S(1)}, f32[3,768]{1,0:T(4,128)S(1)}, u32[]{:S(2)}, u32[]{:S(2)}) collective-permute-start(f32[3,768]{1,0:T(4,128)S(1)} %slice.33), channel_id=1, source_target_pairs={{0,1},{2,3},{4,5},{6,7},{8,9},{10,11},{12,13},{14,15},{16,17},{18,... | collective-permute-start | bytes 27656
  47.9 20.5 %copy-start.9 = (bf16[197,768]{1,0:T(8,128)(2,1)S(1)}, bf16[197,768]{1,0:T(8,128)(2,1)}, u32[]{:S(2)}) copy-start(bf16[197,768]{1,0:T(8,128)(2,1)} %param.23) | copy-start | bytes 907780
  53.1 0.8 copy-start.3
  53.4 18.8 %copy-start.39 = (f32[197]{0:T(256)}, f32[197]{0:T(256)S(1)}, u32[]{:S(2)}) copy-start(f32[197]{0:T(256)S(1)} %multiply_reduce_fusion.6) | copy-start | bytes 2368
  53.4 18.5 %copy-start.25 = (bf16[768,32]{0,1:T(8,128)(2,1)S(1)}, bf16[768,32]{0,1:T(8,128)(2,1)}, u32[]{:S(2)}) copy-start(bf16[768,32]{0,1:T(8,128)(2,1)} %param.19) | copy-start | bytes 147460
  53.9 18.2 %copy-start.34 = (f32[197]{0:T(256)}, f32[197]{0:T(256)S(1)}, u32[]{:S(2)}) copy-start(f32[197]{0:T(256)S(1)} %fusion.67) | copy-start | bytes 2368
  54.1 33.6 %copy-start.11 = (bf16[197,768]{1,0:T(8,128)(2,1)}, bf16[197,768]{1,0:T(8,128)(2,1)S(1)}, u32[]{:S(2)}) copy-start(bf16[197,768]{1,0:T(8,128)(2,1)S(1)} %add_convert_fusion.2) | copy-start | bytes 907780
  60.0 27.7 %all-to-all-start = ((bf16[16,32,768]{2,1,0:T(8,128)(2,1)}), bf16[16,32,768]{2,1,0:T(8,128)(2,1)}, u32[]{:S(2)}, u32[]{:S(2)}) async-start(bf16[16,32,768]{2,1,0:T(8,128)(2,1)} %bitcast.8), calls=%async_computation | async-start | bytes 1572864 | tf_op jit(solution)/shard_map/all_to_all | solution.py:129
  68.3 47.4 %all-gather.5.cloned.1.call-start = ((), (), s32[]{:S(2)}) async-start(), calls=%async_computation.6 | async-start | bytes 2359296 | tf_op jit(solution)/shard_map/all_gather | solution.py:148
  72.2 15.5 %copy-start.36 = (f32[197]{0:T(256)}, f32[197]{0:T(256)S(1)}, u32[]{:S(2)}) copy-start(f32[197]{0:T(256)S(1)} %fusion.55) | copy-start | bytes 2368
  91.2 23.5 %all-to-all-start.2 = ((bf16[16,32,768]{2,1,0:T(8,128)(2,1)}), bf16[16,32,768]{2,1,0:T(8,128)(2,1)S(1)}, u32[]{:S(2)}, u32[]{:S(2)}) async-start(bf16[16,32,768]{2,1,0:T(8,128)(2,1)} %bitcast.107), calls=%async_computation.3 | async-start | bytes 1572864 | tf_op jit(solution)/shard_map/all_to_all | solution.py:136
  96.1 74.9 %all-gather.7.cloned.1.call-start = ((), (), s32[]{:S(2)}) async-start(), calls=%async_computation.8 | async-start | bytes 2359296 | tf_op jit(solution)/shard_map/all_gather | solution.py:149
  114.8 0.9 copy-start.18
  115.7 76.4 %reduce-scatter.7.cloned.1.call-start = ((), (), s32[]{:S(2)}) async-start(), calls=%async_computation.7 | async-start | bytes 2359296 | tf_op jit(solution)/shard_map/reduce_scatter | solution.py:158
  151.0 2.7 copy-start.44
  153.8 32.0 %slice-start = ((s8[4718592]{0:T(1024)(128)(4,1)}), s8[524288]{0:T(1024)(128)(4,1)S(1)}, s32[]{:S(2)}) async-start(s8[4718592]{0:T(1024)(128)(4,1)} %bitcast.114), calls=%async_computation.12 | async-start | bytes 1048576
  162.3 38.5 %reduce-scatter.9.cloned.1.call-start = ((), (), s32[]{:S(2)}) async-start(), calls=%async_computation.9 | async-start | bytes 2359296 | tf_op jit(solution)/shard_map/reduce_scatter | solution.py:168
  171.1 14.7 %slice-start.1 = ((s8[4718592]{0:T(1024)(128)(4,1)}), s8[4194304]{0:T(1024)(128)(4,1)S(1)}, s32[]{:S(2)}) async-start(s8[4718592]{0:T(1024)(128)(4,1)} %bitcast.114), calls=%async_computation.13 | async-start | bytes 8388608
  183.1 2.7 copy-start.43
  192.1 23.9 %all-to-all-start.1 = ((bf16[16,32,768]{2,1,0:T(8,128)(2,1)}), bf16[16,32,768]{2,1,0:T(8,128)(2,1)S(1)}, u32[]{:S(2)}, u32[]{:S(2)}) async-start(bf16[16,32,768]{2,1,0:T(8,128)(2,1)} %bitcast.109), calls=%async_computation.2 | async-start | bytes 1572864 | tf_op jit(solution)/shard_map/all_to_all | solution.py:174
  216.0 23.5 %all-to-all-start.3 = ((bf16[16,32,768]{2,1,0:T(8,128)(2,1)}), bf16[16,32,768]{2,1,0:T(8,128)(2,1)S(1)}, u32[]{:S(2)}, u32[]{:S(2)}) async-start(bf16[16,32,768]{2,1,0:T(8,128)(2,1)} %bitcast.108), calls=%async_computation.5 | async-start | bytes 1572864 | tf_op jit(solution)/shard_map/all_to_all | solution.py:187
  220.9 71.3 %all-reduce.11.cloned.1.call-start = ((), (), s32[]{:S(2)}) async-start(), calls=%async_computation.10 | async-start | bytes 196608 | tf_op jit(solution)/shard_map/psum | solution.py:251
  232.8 15.6 %copy-start.4 = (f32[197,768]{1,0:T(8,128)S(1)}, f32[197,768]{1,0:T(8,128)}, u32[]{:S(2)}) copy-start(f32[197,768]{1,0:T(8,128)} %copy-done.3) | copy-start | bytes 1815556
  242.1 7.6 %copy-start.40 = (f32[197]{0:T(256)S(1)}, f32[197]{0:T(256)}, u32[]{:S(2)}) copy-start(f32[197]{0:T(256)} %copy-done.39) | copy-start | bytes 2368
  242.1 7.7 %copy-start.35 = (f32[197]{0:T(256)S(1)}, f32[197]{0:T(256)}, u32[]{:S(2)}) copy-start(f32[197]{0:T(256)} %copy-done.34) | copy-start | bytes 2368
  242.1 10.5 %copy-start.10 = (bf16[197,768]{1,0:T(8,128)(2,1)S(1)}, bf16[197,768]{1,0:T(8,128)(2,1)}, u32[]{:S(2)}) copy-start(bf16[197,768]{1,0:T(8,128)(2,1)} %param.23) | copy-start | bytes 907780
  251.8 0.8 copy-start.7
  252.8 11.3 %copy-start.14 = (bf16[2,197,6,1,64]{1,4,2,0,3:T(8,128)(2,1)S(1)}, bf16[2,197,6,1,64]{1,4,2,0,3:T(8,128)(2,1)}, u32[]{:S(2)}) copy-start(bf16[2,197,6,1,64]{1,4,2,0,3:T(8,128)(2,1)} %copy-done.13) | copy-start | bytes 907780
  260.9 3.2 copy-start.2
  264.1 1.4 copy-start.16
  264.9 1.1 copy-start.15
  264.9 1.5 copy-start.12
  264.9 2.3 copy-start.20
  270.2 4.7 copy-start.17
  270.2 4.7 copy-start.19
  274.9 208.6 %all-reduce.13.cloned.1.call-start = ((), (), s32[]{:S(2)}) async-start(), calls=%async_computation.11 | async-start | bytes 9633792 | tf_op jit(solution)/shard_map/psum | solution.py:249
  292.1 10.0 %copy-start.23 = (bf16[394,1152]{0,1:T(8,128)(2,1)S(1)}, bf16[394,1152]{0,1:T(8,128)(2,1)}, u32[]{:S(2)}) copy-start(bf16[394,1152]{0,1:T(8,128)(2,1)} %convert_element_type.115) | copy-start | bytes 2723332
  306.8 0.7 copy-start.21
  307.5 14.6 %copy-start.6 = (bf16[197,768]{1,0:T(8,128)(2,1)S(1)}, bf16[197,768]{1,0:T(8,128)(2,1)}, u32[]{:S(2)}) copy-start(bf16[197,768]{1,0:T(8,128)(2,1)} %param.12) | copy-start | bytes 907780
  307.5 14.6 %copy-start.27 = (f32[768]{0:T(1024)S(1)}, f32[768]{0:T(1024)}, u32[]{:S(2)}) copy-start(f32[768]{0:T(1024)} %param.13) | copy-start | bytes 9220
  307.6 14.6 %copy-start.30 = (f32[197]{0:T(256)S(1)}, f32[197]{0:T(256)}, u32[]{:S(2)}) copy-start(f32[197]{0:T(256)} %copy-done.29) | copy-start | bytes 2368
  307.6 14.9 %copy-start.38 = (f32[197]{0:T(256)S(1)}, f32[197]{0:T(256)}, u32[]{:S(2)}) copy-start(f32[197]{0:T(256)} %copy-done.37) | copy-start | bytes 2368
  307.6 14.9 %copy-start.33 = (f32[197]{0:T(256)S(1)}, f32[197]{0:T(256)}, u32[]{:S(2)}) copy-start(f32[197]{0:T(256)} %copy-done.32) | copy-start | bytes 2368
  307.6 97.1 %copy-start.8 = (f32[197,768]{1,0:T(8,128)S(1)}, f32[197,768]{1,0:T(8,128)}, u32[]{:S(2)}) copy-start(f32[197,768]{1,0:T(8,128)} %copy-done.7) | copy-start | bytes 1815556
  307.6 12.5 %collective-permute-start.1 = (bf16[3,768]{1,0:T(4,128)(2,1)S(1)}, bf16[3,768]{1,0:T(4,128)(2,1)S(1)}, u32[]{:S(2)}, u32[]{:S(2)}) collective-permute-start(bf16[3,768]{1,0:T(4,128)(2,1)S(1)} %slice.34), channel_id=1, source_target_pairs={{0,1},{2,3},{4,5},{6,7},{8,9},{10,11},{12,13},{14,15},{16,17},{18,... | collective-permute-start | bytes 13832
  483.5 4.1 copy-start.22
  483.5 5.1 %copy-start.26 = (f32[768,32]{0,1:T(8,128)S(1)}, f32[768,32]{0,1:T(8,128)}, u32[]{:S(2)}) copy-start(f32[768,32]{0,1:T(8,128)} %get-tuple-element.55) | copy-start | bytes 294916
Sparse Core Ops, SparseCore 0:
  87.9 9.0 all-gather.4
  115.8 9.0 all-gather.6
  162.4 8.3 reduce-scatter.6
  192.2 8.5 reduce-scatter.8
  275.0 17.0 all-reduce.10
  298.7 184.7 all-reduce.12
